TPU v7x, 128 devices: a whole 4x4x4 slice. The times are simulated.
128 devices in a mesh: len: 16 (over z, x), xs: 8 (over y, core).
Axes of the slice: x: 4, y: 4, z: 4, core: 2. Of those that a mesh axis runs over, the one named last changes fastest.
Arguments:
- right_side: float32 [3, 16, 64, 16384], P(None, None, None, ('len', 'xs')), may hold values from -19 to 19
- mass_field: float32 [16, 64, 16384], P(None, None, ('len', 'xs')), may hold values from 0.5 to 2
- span_lengths: int32 [128], replicated, may hold values from 1 to 256, 16384 in all
- stick_flags: int32 [256], replicated, may hold values from 0 to 1
- normal_load: float32 [256], replicated, may hold values from 0.5 to 4
- prior_friction: float32 [2, 256], replicated, may hold values from -4 to 4
Outputs:
- increment: float32 [3, 16, 64, 16384], P(None, None, None, ('len', 'xs'))
- residual: float32 [3, 16, 64, 16384], P(None, None, None, ('len', 'xs'))
- friction: float32 [2, 256], replicated
Inputs may be any that keep to these rules, and one draw needn't show every extreme that they name: `span_lengths`: the spans sum to 16384; the longest is exactly 256. `stick_flags`: 1 marks a sticking bearing, 0 a sliding one.
All inputs are finite; a program needn't handle non-finite values.
Results may differ from a plain program's by a relative error of at most 0.0003.
Values sent between devices are 32-bit elements; how exact they have to be, the bound alone decides.
A program may use at most 64 MiB of HBM per device.

v0:
```python
import jax
import jax.numpy as jnp
from jax import lax
from jax.sharding import PartitionSpec as P

ITERS = 3
shear_modulus = 1.0
bulk_modulus = 1.5
elastic_stiffness = 8.0
pendulum_radius = 4.0
vertical_stiffness = 5.0
static_friction = 0.6
kinetic_friction = 0.45


def extended_2(cells, sides, width):
    for axis, dim in sides:
        count = lax.axis_size(axis)
        ends = count - 1
        head = lax.slice_in_dim(cells, 0, width, axis=dim)
        tail = lax.slice_in_dim(cells, cells.shape[dim] - width, cells.shape[dim], axis=dim)
        cells = jnp.concatenate(
            [
                lax.ppermute(tail, axis, [(i, (i + 1) % count) for i in range(ends)]),
                cells,
                lax.ppermute(head, axis, [((i + 1) % count, i) for i in range(ends)]),
            ],
            axis=dim,
        )
    return cells


def window(array, anchor, extent):
    return array[
        ...,
        anchor[0] : anchor[0] + extent[0],
        anchor[1] : anchor[1] + extent[1],
        anchor[2] : anchor[2] + extent[2],
    ]


def shifted(anchor, along_dim, stride):
    moved = list(anchor)
    moved[along_dim] = moved[along_dim] + stride
    return tuple(moved)


def difference(array, anchor, extent, along_dim):
    upper = window(array, shifted(anchor, along_dim, 1), extent)
    lower = window(array, shifted(anchor, along_dim, -1), extent)
    return 0.5 * (upper - lower)


def laplace_at(padded, anchor, extent):
    total = 6.0 * window(padded, anchor, extent)
    for along_dim in range(3):
        for stride in (1, -1):
            total = total - window(padded, shifted(anchor, along_dim, stride), extent)
    return total


def pad_local(array, width):
    widths = [(0, 0)] * array.ndim
    widths[array.ndim - 3] = (width, width)
    widths[array.ndim - 2] = (width, width)
    return jnp.pad(array, widths)


def operate(field, mass_field):
    dims_of = (2, 1, 0)
    extent = field.shape[1:]
    extended = extended_2(field, ((("len", "xs"), 3),), 1)
    extended = pad_local(extended, 1)
    divergence = difference(extended[0], (1, 1, 1), extent, dims_of[0])
    for component in (1, 2):
        divergence = divergence + difference(
            extended[component], (1, 1, 1), extent, dims_of[component]
        )
    div_extended = extended_2(divergence, ((("len", "xs"), 2),), 1)
    div_extended = pad_local(div_extended, 1)
    laplacian = laplace_at(extended, (1, 1, 1), extent)
    gradient = jnp.stack(
        [difference(div_extended, (1, 1, 1), extent, dims_of[c]) for c in range(3)]
    )
    return mass_field[None] * field + shear_modulus * laplacian - bulk_modulus * gradient


def return_map(readout, stick_flags, normal_load, prior_friction):
    coeff = jnp.where(stick_flags == 1, static_friction, kinetic_friction)
    radius = coeff * normal_load
    trial = prior_friction + elastic_stiffness * readout[0:2]
    magnitude = jnp.sqrt(trial[0] * trial[0] + trial[1] * trial[1])
    friction = trial * (radius / jnp.maximum(magnitude, radius))
    horizontal = friction + normal_load / pendulum_radius * readout[0:2]
    vertical = vertical_stiffness * readout[2]
    force = jnp.concatenate([horizontal, vertical[None]], axis=0)
    return (friction, force)


def shards(right_side, mass_field, span_lengths, stick_flags, normal_load, prior_friction):
    local_across = right_side.shape[2]
    local_along = right_side.shape[3]
    bearings = 2 * span_lengths.shape[0]
    ends = jnp.cumsum(span_lengths) - 1
    along_site = jnp.repeat(ends, 2)
    across_site = jnp.tile(
        jnp.array([local_across // 4, 3 * local_across // 4], dtype=jnp.int32),
        span_lengths.shape[0],
    )
    along_start = lax.axis_index(("len", "xs")) * local_along
    along_hit = (
        lax.broadcasted_iota(jnp.int32, (local_along, bearings), 0) + along_start
        == along_site[None, :]
    ).astype(jnp.float32)
    across_hit = (
        lax.broadcasted_iota(jnp.int32, (local_across, bearings), 0) == across_site[None, :]
    ).astype(jnp.float32)
    increment = jnp.zeros_like(right_side)
    solved = right_side
    direction = right_side
    norm_now = lax.psum(jnp.sum(solved * solved), ("len", "xs"))
    for iteration in range(ITERS):
        image = operate(direction, mass_field)
        curvature = lax.psum(jnp.sum(direction * image), ("len", "xs"))
        alpha = norm_now / curvature
        increment = increment + alpha * direction
        solved = solved - alpha * image
        norm_next = lax.psum(jnp.sum(solved * solved), ("len", "xs"))
        direction = solved + norm_next / norm_now * direction
        norm_now = norm_next
    picked = jnp.einsum("csl,lb->csb", increment[:, 0], along_hit, precision=lax.Precision.HIGHEST)
    readout = lax.psum(jnp.sum(picked * across_hit[None], axis=1), ("len", "xs"))
    friction, force = return_map(readout, stick_flags, normal_load, prior_friction)
    spread = force[:, None, :] * across_hit[None]
    placed = jnp.einsum("csb,lb->csl", spread, along_hit, precision=lax.Precision.HIGHEST)
    residual = solved.at[:, 0].add(-placed)
    return (increment, residual, friction)


def solution(mesh):
    in_specs = (
        P(None, None, None, ("len", "xs")),
        P(None, None, ("len", "xs")),
        P(),
        P(),
        P(),
        P(),
    )
    out_specs = (P(None, None, None, ("len", "xs")), P(None, None, None, ("len", "xs")), P())
    return jax.shard_map(shards, mesh=mesh, in_specs=in_specs, out_specs=out_specs, check_vma=False)
```

profile of v0, /device:TPU:1, one launch (start us, length us, event | category | flops | bytes accessed | tf_op | source)
XLA Modules:
  0.0 561.3 jit_solution(11000767857912124190)
XLA Ops:
  0.6 2.6 fusion.70
  3.8 4.6 collective-permute-start
  15.7 3.8 select_maximum_fusion.4
  23.0 3.6 collective-permute-start.3
  26.7 3.9 multiply_reduce_fusion.5
  35.7 76.7 %all-reduce.6 = (f32[]{:T(128)}, f32[]{:T(128)}) all-reduce(f32[]{:T(128)} %get-tuple-element.45, f32[]{:T(128)} %multiply_reduce_fusion.4), channel_id=1, replica_groups=mesh['len'=16,'xs'=8] {'len','xs'}, use_global_device_ids=true, to_apply=%region_1.2 | all-reduce | flops 2 | bytes 16 | tf_op jit(solution)/shard_map/psum | solution.py:121
  113.7 3.6 multiply_reduce_fusion.3
  117.3 64.9 %psum.51 = f32[]{:T(128)} all-reduce(f32[]{:T(128)} %get-tuple-element.30), channel_id=1, replica_groups=mesh['len'=16,'xs'=8] {'len','xs'}, use_global_device_ids=true, to_apply=%region_5.6 | all-reduce | flops 1 | bytes 8 | tf_op jit(solution)/shard_map/psum | solution.py:128
  185.3 2.3 fusion.69
  193.3 2.4 collective-permute-start.5
  200.6 4.1 select_maximum_fusion.2
  208.7 3.6 collective-permute-start.7
  212.4 7.8 %fusion.7 = f32[3,16,64,128]{3,2,1,0:T(8,128)} fusion(f32[3,16,64,128]{3,2,1,0:T(8,128)} %copy.80, f32[3,16,64,1]{3,2,1,0:T(8,128)} %copy.84, f32[3,16,64,1]{3,2,1,0:T(8,128)} %copy.86, f32[3,18,66,130]{3,2,1,0:T(8,128)S(1)} %select_maximum_fusion.2, f32[16,64,128]{2,1,0:T(8,128)S(1)} %copy-done.11), kind=kLoop, calls=%fused_computation.28 | loop fusion | flops 4325376 | bytes 9986048 | tf_op jit(solution)/shard_map/add | solution.py:85
  226.7 74.8 %psum.52 = f32[]{:T(128)} all-reduce(f32[]{:T(128)} %multiply_reduce_fusion.2), channel_id=1, replica_groups=mesh['len'=16,'xs'=8] {'len','xs'}, use_global_device_ids=true, to_apply=%region_7.8 | all-reduce | flops 1 | bytes 8 | tf_op jit(solution)/shard_map/psum | solution.py:124
  302.8 4.7 multiply_reduce_fusion.1
  307.5 62.8 %psum.53 = f32[]{:T(128)} all-reduce(f32[]{:T(128)} %get-tuple-element.28), channel_id=1, replica_groups=mesh['len'=16,'xs'=8] {'len','xs'}, use_global_device_ids=true, to_apply=%region_9.10 | all-reduce | flops 1 | bytes 8 | tf_op jit(solution)/shard_map/psum | solution.py:128
  377.5 2.6 collective-permute-start.9
  382.0 3.0 collective-permute-start.8
  385.0 2.8 copy.94
  391.1 4.3 select_maximum_fusion
  399.6 3.9 collective-permute-start.11
  403.5 7.7 %fusion.4 = f32[3,16,64,128]{3,2,1,0:T(8,128)} fusion(f32[3,16,64,128]{3,2,1,0:T(8,128)} %copy.94, f32[3,16,64,1]{3,2,1,0:T(8,128)} %copy.98, f32[3,16,64,1]{3,2,1,0:T(8,128)} %copy.100, f32[3,18,66,130]{3,2,1,0:T(8,128)S(1)} %select_maximum_fusion, f32[16,64,128]{2,1,0:T(8,128)S(1)} %copy-done.12), kind=kLoop, calls=%fused_computation.19 | loop fusion | flops 4325376 | bytes 9986048 | tf_op jit(solution)/shard_map/add | solution.py:85
  417.2 71.9 %psum.54 = f32[]{:T(128)} all-reduce(f32[]{:T(128)} %multiply_reduce_fusion), channel_id=1, replica_groups=mesh['len'=16,'xs'=8] {'len','xs'}, use_global_device_ids=true, to_apply=%region_11.12 | all-reduce | flops 1 | bytes 8 | tf_op jit(solution)/shard_map/psum | solution.py:124
  495.2 63.5 %psum.55 = f32[3,256]{1,0:T(4,128)S(1)} all-reduce(f32[3,256]{1,0:T(4,128)S(1)} %fusion.16), channel_id=1, replica_groups=mesh['len'=16,'xs'=8] {'len','xs'}, use_global_device_ids=true, to_apply=%region_14.15 | all-reduce | flops 768 | bytes 6144 | tf_op jit(solution)/shard_map/psum | solution.py:132
  (134 shorter events, 67.6 us)
Async XLA Ops:
  3.2 7.6 %copy-start.29 = (s32[2]{0:T(128)S(1)}, s32[2]{0:T(128)}, u32[]{:S(2)}) copy-start(s32[2]{0:T(128)} %constant.71.clone) | copy-start | bytes 28
  3.2 7.8 %copy-start.28 = (s32[128]{0:T(128)S(1)}, s32[128]{0:T(128)}, u32[]{:S(2)}) copy-start(s32[128]{0:T(128)} %param.11) | copy-start | bytes 1540
  3.8 7.5 %collective-permute-start = (f32[3,16,64,1]{2,1,3,0:T(8,128)S(1)}, f32[3,16,64,1]{2,1,3,0:T(8,128)S(1)}, u32[]{:S(2)}, u32[]{:S(2)}) collective-permute-start(f32[3,16,64,1]{2,1,3,0:T(8,128)S(1)} %copy.111), channel_id=1, source_target_pairs={{0,1},{1,2},{2,3},{3,4},{4,5},{5,6},{6,7},{7,8},{8,9},{9,10},{10,1... | collective-permute-start | bytes 36872 | tf_op jit(solution)/shard_map/ppermute | solution.py:24
  8.9 5.2 collective-permute-start.1
  11.3 4.4 copy-start
  11.8 7.7 %copy-start.6 = (f32[3,16,64,1]{3,2,1,0:T(8,128)}, f32[3,16,64,1]{3,2,1,0:T(8,128)S(1)}, u32[]{:S(2)}) copy-start(f32[3,16,64,1]{3,2,1,0:T(8,128)S(1)} %copy.70) | copy-start | bytes 36868
  19.9 6.8 %copy-start.8 = (f32[3,16,64,1]{3,2,1,0:T(8,128)S(1)}, f32[3,16,64,1]{3,2,1,0:T(8,128)}, u32[]{:S(2)}) copy-start(f32[3,16,64,1]{3,2,1,0:T(8,128)} %copy.71) | copy-start | bytes 36868
  20.8 6.0 %copy-start.7 = (f32[3,16,64,1]{3,2,1,0:T(8,128)S(1)}, f32[3,16,64,1]{3,2,1,0:T(8,128)}, u32[]{:S(2)}) copy-start(f32[3,16,64,1]{3,2,1,0:T(8,128)} %copy-done.6) | copy-start | bytes 36868
  20.8 6.0 %copy-start.10 = (f32[16,64,128]{2,1,0:T(8,128)S(1)}, f32[16,64,128]{2,1,0:T(8,128)}, u32[]{:S(2)}) copy-start(f32[16,64,128]{2,1,0:T(8,128)} %param.10) | copy-start | bytes 1572868
  21.0 10.6 %collective-permute-start.2 = (f32[16,64,1]{2,1,0:T(8,128)S(1)}, f32[16,64,1]{2,1,0:T(8,128)S(1)}, u32[]{:S(2)}, u32[]{:S(2)}) collective-permute-start(f32[16,64,1]{2,1,0:T(8,128)S(1)} %get-tuple-element.60), channel_id=1, source_target_pairs={{1,0},{2,1},{3,2},{4,3},{5,4},{6,5},{7,6},{8,7},{9,8},{10,9},{11,1... | collective-permute-start | bytes 12296 | tf_op jit(solution)/shard_map/ppermute | solution.py:26
  23.0 9.8 %collective-permute-start.3 = (f32[16,64,1]{2,1,0:T(8,128)S(1)}, f32[16,64,1]{2,1,0:T(8,128)S(1)}, u32[]{:S(2)}, u32[]{:S(2)}) collective-permute-start(f32[16,64,1]{2,1,0:T(8,128)S(1)} %get-tuple-element.59), channel_id=1, source_target_pairs={{0,1},{1,2},{2,3},{3,4},{4,5},{5,6},{6,7},{7,8},{8,9},{9,10},{10,1... | collective-permute-start | bytes 12296 | tf_op jit(solution)/shard_map/ppermute | solution.py:24
  189.5 7.7 %collective-permute-start.4 = (f32[3,16,64,1]{2,1,3,0:T(8,128)S(1)}, f32[3,16,64,1]{2,1,3,0:T(8,128)S(1)}, u32[]{:S(2)}, u32[]{:S(2)}) collective-permute-start(f32[3,16,64,1]{2,1,3,0:T(8,128)S(1)} %copy.82), channel_id=1, source_target_pairs={{0,1},{1,2},{2,3},{3,4},{4,5},{5,6},{6,7},{7,8},{8,9},{9,10},{10,1... | collective-permute-start | bytes 36872 | tf_op jit(solution)/shard_map/ppermute | solution.py:24
  193.3 5.5 collective-permute-start.5
  205.7 6.7 %copy-start.11 = (f32[16,64,128]{2,1,0:T(8,128)S(1)}, f32[16,64,128]{2,1,0:T(8,128)}, u32[]{:S(2)}) copy-start(f32[16,64,128]{2,1,0:T(8,128)} %param.10) | copy-start | bytes 1572868
  206.8 13.4 %collective-permute-start.6 = (f32[16,64,1]{2,1,0:T(8,128)}, f32[16,64,1]{2,1,0:T(8,128)}, u32[]{:S(2)}, u32[]{:S(2)}) collective-permute-start(f32[16,64,1]{2,1,0:T(8,128)} %get-tuple-element.58), channel_id=1, source_target_pairs={{1,0},{2,1},{3,2},{4,3},{5,4},{6,5},{7,6},{8,7},{9,8},{10,9},{11,1... | collective-permute-start | bytes 12296 | tf_op jit(solution)/shard_map/ppermute | solution.py:26
  208.7 11.4 %collective-permute-start.7 = (f32[16,64,1]{2,1,0:T(8,128)}, f32[16,64,1]{2,1,0:T(8,128)}, u32[]{:S(2)}, u32[]{:S(2)}) collective-permute-start(f32[16,64,1]{2,1,0:T(8,128)} %get-tuple-element.57), channel_id=1, source_target_pairs={{0,1},{1,2},{2,3},{3,4},{4,5},{5,6},{6,7},{7,8},{8,9},{9,10},{10,1... | collective-permute-start | bytes 12296 | tf_op jit(solution)/shard_map/ppermute | solution.py:24
  377.5 10.3 %collective-permute-start.9 = (f32[3,16,64,1]{2,1,3,0:T(8,128)S(1)}, f32[3,16,64,1]{2,1,3,0:T(8,128)S(1)}, u32[]{:S(2)}, u32[]{:S(2)}) collective-permute-start(f32[3,16,64,1]{2,1,3,0:T(8,128)S(1)} %copy.97), channel_id=1, source_target_pairs={{1,0},{2,1},{3,2},{4,3},{5,4},{6,5},{7,6},{8,7},{9,8},{10,9},{11,1... | collective-permute-start | bytes 36872 | tf_op jit(solution)/shard_map/ppermute | solution.py:26
  382.0 7.5 %collective-permute-start.8 = (f32[3,16,64,1]{2,1,3,0:T(8,128)S(1)}, f32[3,16,64,1]{2,1,3,0:T(8,128)S(1)}, u32[]{:S(2)}, u32[]{:S(2)}) collective-permute-start(f32[3,16,64,1]{2,1,3,0:T(8,128)S(1)} %copy.96), channel_id=1, source_target_pairs={{0,1},{1,2},{2,3},{3,4},{4,5},{5,6},{6,7},{7,8},{8,9},{9,10},{10,1... | collective-permute-start | bytes 36872 | tf_op jit(solution)/shard_map/ppermute | solution.py:24
  396.5 7.0 %copy-start.12 = (f32[16,64,128]{2,1,0:T(8,128)S(1)}, f32[16,64,128]{2,1,0:T(8,128)}, u32[]{:S(2)}) copy-start(f32[16,64,128]{2,1,0:T(8,128)} %param.10) | copy-start | bytes 1572868
  397.7 13.4 %collective-permute-start.10 = (f32[16,64,1]{2,1,0:T(8,128)}, f32[16,64,1]{2,1,0:T(8,128)}, u32[]{:S(2)}, u32[]{:S(2)}) collective-permute-start(f32[16,64,1]{2,1,0:T(8,128)} %get-tuple-element.56), channel_id=1, source_target_pairs={{1,0},{2,1},{3,2},{4,3},{5,4},{6,5},{7,6},{8,7},{9,8},{10,9},{11,1... | collective-permute-start | bytes 12296 | tf_op jit(solution)/shard_map/ppermute | solution.py:26
  399.6 11.5 %collective-permute-start.11 = (f32[16,64,1]{2,1,0:T(8,128)}, f32[16,64,1]{2,1,0:T(8,128)}, u32[]{:S(2)}, u32[]{:S(2)}) collective-permute-start(f32[16,64,1]{2,1,0:T(8,128)} %get-tuple-element.55), channel_id=1, source_target_pairs={{0,1},{1,2},{2,3},{3,4},{4,5},{5,6},{6,7},{7,8},{8,9},{9,10},{10,1... | collective-permute-start | bytes 12296 | tf_op jit(solution)/shard_map/ppermute | solution.py:24
  493.6 65.1 %copy-start.25 = (f32[2,256]{1,0:T(2,128)S(1)}, f32[2,256]{1,0:T(2,128)}, u32[]{:S(2)}) copy-start(f32[2,256]{1,0:T(2,128)} %param.14) | copy-start | bytes 6148
  493.6 65.1 %copy-start.26 = (f32[256]{0:T(256)S(1)}, f32[256]{0:T(256)}, u32[]{:S(2)}) copy-start(f32[256]{0:T(256)} %param.13) | copy-start | bytes 3076
  493.7 65.1 %copy-start.27 = (s32[256]{0:T(256)S(1)}, s32[256]{0:T(256)}, u32[]{:S(2)}) copy-start(s32[256]{0:T(256)} %param.12) | copy-start | bytes 3076
  (18 other events, 39.7 us)
where the time goes:
time: 570 us; the launch traced here: 561 us
  blocking collectives  414 us (73%)
  other arithmetic  63.3 us (11%)
  local copies, waits for them, and re-layouts  36.9 us (6%)
  starting transfers between devices  33.4 us (6%)
  between operations  8.1 us (1%)
    psum x2, blocking collectives, shards(): curvature = lax.psum(jnp.sum(direction * image), ('len', 'xs'))  147 us
    psum x2, blocking collectives, shards(): norm_next = lax.psum(jnp.sum(solved * solved), ('len', 'xs'))  128 us
    psum x1, blocking collectives, shards(): norm_now = lax.psum(jnp.sum(solved * solved), ('len', 'xs'))  76.7 us
    psum x1, blocking collectives, shards(): lax.psum(jnp.sum(picked * across_hit[None], axis=1), ('len', 'xs'))  63.5 us
    ppermute x6, starting transfers between devices, extended_2(): lax.ppermute(tail, axis, [(i, (i + 1) % count) for i in range(ends)])  20.7 us
    concatenate x6, other arithmetic, extended_2(): jnp.concatenate([lax.ppermute(tail, axis, [(i, (i + 1) % count) for i in...  16.2 us
    add x2, other arithmetic, operate(): mass_field[None] * field + shear_modulus * laplacian  15.4 us
    slice x8, local copies, waits for them, and re-layouts, extended_2(): lax.slice_in_dim(cells, cells.shape[dim] - width, cells.shape[dim], axis=...  13.4 us
  transfers between devices with their start and end apart: 12, of which 3 were waited for; matrix products, arithmetic and copies ran while one was open for 6% of the time, Pallas kernels for 0%

commit v1 on v0

--- a/solution.py
+++ b/solution.py
@@ -129,7 +129,9 @@
         direction = solved + norm_next / norm_now * direction
         norm_now = norm_next
     picked = jnp.einsum("csl,lb->csb", increment[:, 0], along_hit, precision=lax.Precision.HIGHEST)
-    readout = lax.psum(jnp.sum(picked * across_hit[None], axis=1), ("len", "xs"))
+    readout = jnp.sum(
+        lax.all_gather(jnp.sum(picked * across_hit[None], axis=1), ("len", "xs")), axis=0
+    )
     friction, force = return_map(readout, stick_flags, normal_load, prior_friction)
     spread = force[:, None, :] * across_hit[None]
     placed = jnp.einsum("csb,lb->csl", spread, along_hit, precision=lax.Precision.HIGHEST)

time: 570 us -> 541 us (0.949)
  blocking collectives: 414 us -> 386 us
    psum x1 -> x0, blocking collectives: 63.5 us -> none  [shards(): lax.psum(jnp.sum(picked * across_hit[None], axis=1), ('len', 'xs'))]
    all_gather x0 -> x1, blocking collectives: none -> 34.5 us  [shards(): lax.all_gather(jnp.sum(picked * across_hit[None], axis=1), ('len', 'xs'))]
where the time goes in v1:
time: 541 us; the launch traced here: 532 us
  blocking collectives  386 us (71%)
  other arithmetic  63.5 us (12%)
  local copies, waits for them, and re-layouts  36.9 us (7%)
  starting transfers between devices  33.4 us (6%)
  between operations  8.11 us (1%)
    psum x2, blocking collectives, shards(): curvature = lax.psum(jnp.sum(direction * image), ('len', 'xs'))  147 us
    psum x2, blocking collectives, shards(): norm_next = lax.psum(jnp.sum(solved * solved), ('len', 'xs'))  128 us
    psum x1, blocking collectives, shards(): norm_now = lax.psum(jnp.sum(solved * solved), ('len', 'xs'))  76.7 us
    all_gather x1, blocking collectives, shards(): lax.all_gather(jnp.sum(picked * across_hit[None], axis=1), ('len', 'xs'))  34.5 us
    ppermute x6, starting transfers between devices, extended_2(): lax.ppermute(tail, axis, [(i, (i + 1) % count) for i in range(ends)])  20.7 us
    concatenate x6, other arithmetic, extended_2(): jnp.concatenate([lax.ppermute(tail, axis, [(i, (i + 1) % count) for i in...  16.2 us
    add x2, other arithmetic, operate(): mass_field[None] * field + shear_modulus * laplacian  15.4 us
    slice x8, local copies, waits for them, and re-layouts, extended_2(): lax.slice_in_dim(cells, cells.shape[dim] - width, cells.shape[dim], axis=...  13.4 us
  transfers between devices with their start and end apart: 12, of which 3 were waited for; matrix products, arithmetic and copies ran while one was open for 6% of the time, Pallas kernels for 0%

profile of v1, /device:TPU:1, one launch (start us, length us, event | category | flops | bytes accessed | tf_op | source)
XLA Modules:
  0.0 532.5 jit_solution(12798461597493720446)
XLA Ops:
  0.6 2.6 fusion.70
  3.8 4.6 collective-permute-start
  15.7 3.8 select_maximum_fusion.4
  23.0 3.6 collective-permute-start.3
  26.7 3.9 multiply_reduce_fusion.5
  35.7 76.7 %all-reduce.6 = (f32[]{:T(128)}, f32[]{:T(128)}) all-reduce(f32[]{:T(128)} %get-tuple-element.45, f32[]{:T(128)} %multiply_reduce_fusion.4), channel_id=1, replica_groups=mesh['len'=16,'xs'=8] {'len','xs'}, use_global_device_ids=true, to_apply=%region_1.2 | all-reduce | flops 2 | bytes 16 | tf_op jit(solution)/shard_map/psum | solution.py:121
  113.7 3.6 multiply_reduce_fusion.3
  117.3 64.9 %psum.44 = f32[]{:T(128)} all-reduce(f32[]{:T(128)} %get-tuple-element.30), channel_id=1, replica_groups=mesh['len'=16,'xs'=8] {'len','xs'}, use_global_device_ids=true, to_apply=%region_5.6 | all-reduce | flops 1 | bytes 8 | tf_op jit(solution)/shard_map/psum | solution.py:128
  185.3 2.3 fusion.69
  193.3 2.4 collective-permute-start.5
  200.6 4.1 select_maximum_fusion.2
  208.7 3.6 collective-permute-start.7
  212.4 7.8 %fusion.7 = f32[3,16,64,128]{3,2,1,0:T(8,128)} fusion(f32[3,16,64,128]{3,2,1,0:T(8,128)} %copy.80, f32[3,16,64,1]{3,2,1,0:T(8,128)} %copy.84, f32[3,16,64,1]{3,2,1,0:T(8,128)} %copy.86, f32[3,18,66,130]{3,2,1,0:T(8,128)S(1)} %select_maximum_fusion.2, f32[16,64,128]{2,1,0:T(8,128)S(1)} %copy-done.11), kind=kLoop, calls=%fused_computation.28 | loop fusion | flops 4325376 | bytes 9986048 | tf_op jit(solution)/shard_map/add | solution.py:85
  226.7 74.8 %psum.45 = f32[]{:T(128)} all-reduce(f32[]{:T(128)} %multiply_reduce_fusion.2), channel_id=1, replica_groups=mesh['len'=16,'xs'=8] {'len','xs'}, use_global_device_ids=true, to_apply=%region_7.8 | all-reduce | flops 1 | bytes 8 | tf_op jit(solution)/shard_map/psum | solution.py:124
  302.8 4.7 multiply_reduce_fusion.1
  307.5 62.8 %psum.46 = f32[]{:T(128)} all-reduce(f32[]{:T(128)} %get-tuple-element.28), channel_id=1, replica_groups=mesh['len'=16,'xs'=8] {'len','xs'}, use_global_device_ids=true, to_apply=%region_9.10 | all-reduce | flops 1 | bytes 8 | tf_op jit(solution)/shard_map/psum | solution.py:128
  377.5 2.6 collective-permute-start.9
  382.0 3.0 collective-permute-start.8
  385.0 2.8 copy.94
  391.1 4.3 select_maximum_fusion
  399.6 3.9 collective-permute-start.11
  403.5 7.7 %fusion.4 = f32[3,16,64,128]{3,2,1,0:T(8,128)} fusion(f32[3,16,64,128]{3,2,1,0:T(8,128)} %copy.94, f32[3,16,64,1]{3,2,1,0:T(8,128)} %copy.98, f32[3,16,64,1]{3,2,1,0:T(8,128)} %copy.100, f32[3,18,66,130]{3,2,1,0:T(8,128)S(1)} %select_maximum_fusion, f32[16,64,128]{2,1,0:T(8,128)S(1)} %copy-done.12), kind=kLoop, calls=%fused_computation.19 | loop fusion | flops 4325376 | bytes 9986048 | tf_op jit(solution)/shard_map/add | solution.py:85
  417.2 71.9 %psum.47 = f32[]{:T(128)} all-reduce(f32[]{:T(128)} %multiply_reduce_fusion), channel_id=1, replica_groups=mesh['len'=16,'xs'=8] {'len','xs'}, use_global_device_ids=true, to_apply=%region_11.12 | all-reduce | flops 1 | bytes 8 | tf_op jit(solution)/shard_map/psum | solution.py:124
  495.2 34.5 %all-gather.1 = f32[128,3,256]{2,1,0:T(4,128)S(1)} all-gather(f32[1,3,256]{2,1,0:T(4,128)S(1)} %bitcast.57), channel_id=2, replica_groups=mesh['len'=16,'xs'=8] {'len','xs'}, dimensions={0}, use_global_device_ids=true | all-gather | bytes 396288 | tf_op jit(solution)/shard_map/all_gather | solution.py:133
  (135 shorter events, 67.7 us)
Async XLA Ops:
  3.2 7.6 %copy-start.29 = (s32[2]{0:T(128)S(1)}, s32[2]{0:T(128)}, u32[]{:S(2)}) copy-start(s32[2]{0:T(128)} %constant.71.clone) | copy-start | bytes 28
  3.2 7.8 %copy-start.28 = (s32[128]{0:T(128)S(1)}, s32[128]{0:T(128)}, u32[]{:S(2)}) copy-start(s32[128]{0:T(128)} %param.11) | copy-start | bytes 1540
  3.8 7.5 %collective-permute-start = (f32[3,16,64,1]{2,1,3,0:T(8,128)S(1)}, f32[3,16,64,1]{2,1,3,0:T(8,128)S(1)}, u32[]{:S(2)}, u32[]{:S(2)}) collective-permute-start(f32[3,16,64,1]{2,1,3,0:T(8,128)S(1)} %copy.111), channel_id=1, source_target_pairs={{0,1},{1,2},{2,3},{3,4},{4,5},{5,6},{6,7},{7,8},{8,9},{9,10},{10,1... | collective-permute-start | bytes 36872 | tf_op jit(solution)/shard_map/ppermute | solution.py:24
  8.9 5.2 collective-permute-start.1
  11.3 4.4 copy-start
  11.8 7.7 %copy-start.6 = (f32[3,16,64,1]{3,2,1,0:T(8,128)}, f32[3,16,64,1]{3,2,1,0:T(8,128)S(1)}, u32[]{:S(2)}) copy-start(f32[3,16,64,1]{3,2,1,0:T(8,128)S(1)} %copy.70) | copy-start | bytes 36868
  19.9 6.8 %copy-start.8 = (f32[3,16,64,1]{3,2,1,0:T(8,128)S(1)}, f32[3,16,64,1]{3,2,1,0:T(8,128)}, u32[]{:S(2)}) copy-start(f32[3,16,64,1]{3,2,1,0:T(8,128)} %copy.71) | copy-start | bytes 36868
  20.8 6.0 %copy-start.7 = (f32[3,16,64,1]{3,2,1,0:T(8,128)S(1)}, f32[3,16,64,1]{3,2,1,0:T(8,128)}, u32[]{:S(2)}) copy-start(f32[3,16,64,1]{3,2,1,0:T(8,128)} %copy-done.6) | copy-start | bytes 36868
  20.8 6.0 %copy-start.10 = (f32[16,64,128]{2,1,0:T(8,128)S(1)}, f32[16,64,128]{2,1,0:T(8,128)}, u32[]{:S(2)}) copy-start(f32[16,64,128]{2,1,0:T(8,128)} %param.10) | copy-start | bytes 1572868
  21.0 10.6 %collective-permute-start.2 = (f32[16,64,1]{2,1,0:T(8,128)S(1)}, f32[16,64,1]{2,1,0:T(8,128)S(1)}, u32[]{:S(2)}, u32[]{:S(2)}) collective-permute-start(f32[16,64,1]{2,1,0:T(8,128)S(1)} %get-tuple-element.60), channel_id=1, source_target_pairs={{1,0},{2,1},{3,2},{4,3},{5,4},{6,5},{7,6},{8,7},{9,8},{10,9},{11,1... | collective-permute-start | bytes 12296 | tf_op jit(solution)/shard_map/ppermute | solution.py:26
  23.0 9.8 %collective-permute-start.3 = (f32[16,64,1]{2,1,0:T(8,128)S(1)}, f32[16,64,1]{2,1,0:T(8,128)S(1)}, u32[]{:S(2)}, u32[]{:S(2)}) collective-permute-start(f32[16,64,1]{2,1,0:T(8,128)S(1)} %get-tuple-element.59), channel_id=1, source_target_pairs={{0,1},{1,2},{2,3},{3,4},{4,5},{5,6},{6,7},{7,8},{8,9},{9,10},{10,1... | collective-permute-start | bytes 12296 | tf_op jit(solution)/shard_map/ppermute | solution.py:24
  189.5 7.7 %collective-permute-start.4 = (f32[3,16,64,1]{2,1,3,0:T(8,128)S(1)}, f32[3,16,64,1]{2,1,3,0:T(8,128)S(1)}, u32[]{:S(2)}, u32[]{:S(2)}) collective-permute-start(f32[3,16,64,1]{2,1,3,0:T(8,128)S(1)} %copy.82), channel_id=1, source_target_pairs={{0,1},{1,2},{2,3},{3,4},{4,5},{5,6},{6,7},{7,8},{8,9},{9,10},{10,1... | collective-permute-start | bytes 36872 | tf_op jit(solution)/shard_map/ppermute | solution.py:24
  193.3 5.5 %collective-permute-start.5 = (f32[3,16,64,1]{2,1,3,0:T(8,128)S(1)}, f32[3,16,64,1]{2,1,3,0:T(8,128)S(1)}, u32[]{:S(2)}, u32[]{:S(2)}) collective-permute-start(f32[3,16,64,1]{2,1,3,0:T(8,128)S(1)} %copy.83), channel_id=1, source_target_pairs={{1,0},{2,1},{3,2},{4,3},{5,4},{6,5},{7,6},{8,7},{9,8},{10,9},{11,1... | collective-permute-start | bytes 36872 | tf_op jit(solution)/shard_map/ppermute | solution.py:26
  205.7 6.7 %copy-start.11 = (f32[16,64,128]{2,1,0:T(8,128)S(1)}, f32[16,64,128]{2,1,0:T(8,128)}, u32[]{:S(2)}) copy-start(f32[16,64,128]{2,1,0:T(8,128)} %param.10) | copy-start | bytes 1572868
  206.8 13.4 %collective-permute-start.6 = (f32[16,64,1]{2,1,0:T(8,128)}, f32[16,64,1]{2,1,0:T(8,128)}, u32[]{:S(2)}, u32[]{:S(2)}) collective-permute-start(f32[16,64,1]{2,1,0:T(8,128)} %get-tuple-element.58), channel_id=1, source_target_pairs={{1,0},{2,1},{3,2},{4,3},{5,4},{6,5},{7,6},{8,7},{9,8},{10,9},{11,1... | collective-permute-start | bytes 12296 | tf_op jit(solution)/shard_map/ppermute | solution.py:26
  208.7 11.4 %collective-permute-start.7 = (f32[16,64,1]{2,1,0:T(8,128)}, f32[16,64,1]{2,1,0:T(8,128)}, u32[]{:S(2)}, u32[]{:S(2)}) collective-permute-start(f32[16,64,1]{2,1,0:T(8,128)} %get-tuple-element.57), channel_id=1, source_target_pairs={{0,1},{1,2},{2,3},{3,4},{4,5},{5,6},{6,7},{7,8},{8,9},{9,10},{10,1... | collective-permute-start | bytes 12296 | tf_op jit(solution)/shard_map/ppermute | solution.py:24
  377.5 10.3 %collective-permute-start.9 = (f32[3,16,64,1]{2,1,3,0:T(8,128)S(1)}, f32[3,16,64,1]{2,1,3,0:T(8,128)S(1)}, u32[]{:S(2)}, u32[]{:S(2)}) collective-permute-start(f32[3,16,64,1]{2,1,3,0:T(8,128)S(1)} %copy.97), channel_id=1, source_target_pairs={{1,0},{2,1},{3,2},{4,3},{5,4},{6,5},{7,6},{8,7},{9,8},{10,9},{11,1... | collective-permute-start | bytes 36872 | tf_op jit(solution)/shard_map/ppermute | solution.py:26
  382.0 7.5 %collective-permute-start.8 = (f32[3,16,64,1]{2,1,3,0:T(8,128)S(1)}, f32[3,16,64,1]{2,1,3,0:T(8,128)S(1)}, u32[]{:S(2)}, u32[]{:S(2)}) collective-permute-start(f32[3,16,64,1]{2,1,3,0:T(8,128)S(1)} %copy.96), channel_id=1, source_target_pairs={{0,1},{1,2},{2,3},{3,4},{4,5},{5,6},{6,7},{7,8},{8,9},{9,10},{10,1... | collective-permute-start | bytes 36872 | tf_op jit(solution)/shard_map/ppermute | solution.py:24
  396.5 7.0 %copy-start.12 = (f32[16,64,128]{2,1,0:T(8,128)S(1)}, f32[16,64,128]{2,1,0:T(8,128)}, u32[]{:S(2)}) copy-start(f32[16,64,128]{2,1,0:T(8,128)} %param.10) | copy-start | bytes 1572868
  397.7 13.4 %collective-permute-start.10 = (f32[16,64,1]{2,1,0:T(8,128)}, f32[16,64,1]{2,1,0:T(8,128)}, u32[]{:S(2)}, u32[]{:S(2)}) collective-permute-start(f32[16,64,1]{2,1,0:T(8,128)} %get-tuple-element.56), channel_id=1, source_target_pairs={{1,0},{2,1},{3,2},{4,3},{5,4},{6,5},{7,6},{8,7},{9,8},{10,9},{11,1... | collective-permute-start | bytes 12296 | tf_op jit(solution)/shard_map/ppermute | solution.py:26
  399.6 11.5 %collective-permute-start.11 = (f32[16,64,1]{2,1,0:T(8,128)}, f32[16,64,1]{2,1,0:T(8,128)}, u32[]{:S(2)}, u32[]{:S(2)}) collective-permute-start(f32[16,64,1]{2,1,0:T(8,128)} %get-tuple-element.55), channel_id=1, source_target_pairs={{0,1},{1,2},{2,3},{3,4},{4,5},{5,6},{6,7},{7,8},{8,9},{9,10},{10,1... | collective-permute-start | bytes 12296 | tf_op jit(solution)/shard_map/ppermute | solution.py:24
  493.6 36.3 %copy-start.25 = (f32[2,256]{1,0:T(2,128)S(1)}, f32[2,256]{1,0:T(2,128)}, u32[]{:S(2)}) copy-start(f32[2,256]{1,0:T(2,128)} %param.14) | copy-start | bytes 6148
  493.6 36.3 %copy-start.26 = (f32[256]{0:T(256)S(1)}, f32[256]{0:T(256)}, u32[]{:S(2)}) copy-start(f32[256]{0:T(256)} %param.13) | copy-start | bytes 3076
  493.7 36.3 %copy-start.27 = (s32[256]{0:T(256)S(1)}, s32[256]{0:T(256)}, u32[]{:S(2)}) copy-start(s32[256]{0:T(256)} %param.12) | copy-start | bytes 3076
  (18 other events, 39.7 us)
